TPU v7x, 32 devices: a whole 2x2x4 slice. The times are simulated.
32 devices in a mesh: gx: 2 (over y), gy: 4 (over x, core), gz: 4 (over z).
Axes of the slice: x: 2, y: 2, z: 4, core: 2. Of those that a mesh axis runs over, the one named last changes fastest.
Arguments:
- snapshot: float32 [12, 1024, 8, 512], P(None, 'gz', 'gx', 'gy'), may hold values from -108 to 108
- species_pick: int32 [8], replicated, may hold values from 0 to 11, as said below
- basis_start: float32 [1024, 384], replicated, may hold values from -0.1875 to 0.1875
Outputs:
- gram_matrix: float32 [1024, 1024], P(('gx', 'gy', 'gz'))
- basis: float32 [1024, 384], P(('gx', 'gy', 'gz'))
- core_tensor: float32 [8, 384, 8, 512], P(None, None, ('gx', 'gz'), 'gy')
Inputs may be any that keep to these rules, and one draw needn't show every extreme that they name: `species_pick`: 8 distinct species numbers; 0 and 11 are always among them.
All inputs are finite; a program needn't handle non-finite values.
Results may differ from a plain program's by a relative error of at most 0.0003.
Values sent between devices are 32-bit elements; how exact they have to be, the bound alone decides.
A program may use at most 128 MiB of HBM per device.

v0:
```python
import jax
import jax.numpy as jnp
from jax import lax
from jax.sharding import PartitionSpec as P


def per_device(snapshot, species_pick, basis_start):
    highest = lax.Precision.HIGHEST
    picked = jnp.take(snapshot, species_pick, axis=0)
    full_panel = lax.all_to_all(picked, "gz", split_axis=2, concat_axis=1, tiled=True)
    total_rows = full_panel.shape[1]
    column_total = (
        full_panel.shape[0]
        * full_panel.shape[2]
        * lax.axis_size("gz")
        * lax.axis_size("gx")
        * full_panel.shape[3]
        * lax.axis_size("gy")
    )
    scaling = 1.0 / column_total
    row_share = total_rows // lax.axis_size(("gx", "gy", "gz"))
    gram_full = lax.psum(
        jnp.einsum("sxyz,swyz->xw", full_panel, full_panel, precision=highest) * scaling,
        ("gx", "gy", "gz"),
    )
    image_full = jnp.dot(gram_full, basis_start, precision=highest)
    inner_gram = jnp.einsum("xr,xq->rq", image_full, image_full, precision=highest)
    lower_factor = jnp.linalg.cholesky(inner_gram)
    basis_full = jax.scipy.linalg.solve_triangular(lower_factor, image_full.T, lower=True).T
    offset = lax.axis_index(("gx", "gy", "gz")) * row_share
    gram_rows = lax.dynamic_slice_in_dim(gram_full, offset, row_share, 0)
    basis_rows = lax.dynamic_slice_in_dim(basis_full, offset, row_share, 0)
    local_rows = picked.shape[1]
    own_rows = lax.dynamic_slice_in_dim(
        basis_full, lax.axis_index("gz") * local_rows, local_rows, 0
    )
    projected = jnp.einsum("xr,sxyz->sryz", own_rows, picked, precision=highest)
    core_out = lax.psum_scatter(projected, "gz", scatter_dimension=2, tiled=True)
    return (gram_rows, basis_rows, core_out)


def solution(mesh):
    return jax.shard_map(
        per_device,
        mesh=mesh,
        in_specs=(P(None, "gz", "gx", "gy"), P(), P()),
        out_specs=(
            P(("gx", "gy", "gz"), None),
            P(("gx", "gy", "gz"), None),
            P(None, None, ("gx", "gz"), "gy"),
        ),
        check_vma=False,
    )
```

profile of v0, /device:TPU:0, one launch (start us, length us, event | category | flops | bytes accessed | tf_op | source)
XLA Modules:
  0.0 657.8 jit_solution(451371687744276982)
XLA Ops:
  8.7 7.5 %gather_fusion = f32[8,256,4,128]{3,2,1,0:T(4,128)} fusion(f32[12,256,4,128]{3,2,1,0:T(4,128)} %param.3, s32[1024]{0:T(1024)S(1)} %pad_clamp_fusion), kind=kCustom, calls=%fused_computation | custom fusion | bytes 8388640 | tf_op jit(solution)/shard_map/jit(_take)/gather | solution.py:9
  16.2 3.3 broadcast_select_fusion
  21.4 99.2 %all_to_all.15 = f32[8,256,4,128]{3,1,0,2:T(8,128)S(1)} all-to-all(f32[8,256,4,128]{3,1,0,2:T(8,128)S(1)} %copy.16), channel_id=1, replica_groups=mesh['gx'=2,'gy'=4,'gz'=4] {'gz'}, dimensions={2} | all-to-all | bytes 8388608 | tf_op jit(solution)/shard_map/all_to_all | solution.py:10
  121.1 14.8 %bitcast_multiply_fusion = f32[1024,1024]{1,0:T(8,128)} fusion(f32[8,1024,128]{2,1,0:T(8,128)S(1)} %bitcast.74), kind=kOutput, calls=%fused_computation.3 | convolution fusion | flops 12885950464 | bytes 8388608 | tf_op jit(solution)/shard_map/sxyz,swyz->xw/dot_general | solution.py:23
  136.1 141.0 %all-reduce.5.cloned.1.call-done = f32[1024,1024]{1,0:T(8,128)} async-done(((f32[1024,1024]{1,0:T(8,128)}), f32[1024,1024]{1,0:T(8,128)}) %all-reduce.5.cloned.1.call-update) | async-done | bytes 4194320 | tf_op jit(solution)/shard_map/psum | solution.py:22
  277.2 8.5 %fusion.27 = f32[1024,384]{1,0:T(8,128)S(1)} fusion(f32[1024,1024]{1,0:T(8,128)} %all-reduce.5.cloned.1.call-done, f32[1024,384]{1,0:T(8,128)S(1)} %copy-done), kind=kOutput, calls=%fused_computation.62 | convolution fusion | flops 4831838208 | bytes 7340032 | tf_op jit(solution)/shard_map/dot_general | solution.py:26
  285.7 3.5 fusion.28
  289.2 2.1 copy.18
  293.5 11.7 %cholesky.77 = f32[128,128]{1,0:T(8,128)S(1)} custom-call(f32[128,128]{1,0:T(8,128)S(1)} %cholesky.192), custom_call_target="Cholesky" | custom-call | tf_op jit(solution)/shard_map/jit(cholesky)/cholesky | solution.py:28
  306.1 9.8 %custom-call.23 = f32[1,128,128]{1,2,0:T(8,128)S(1)} custom-call(f32[1,128,128]{2,1,0:T(8,128)S(1)} %get-tuple-element.36), custom_call_target="InvertDiagBlocksLowerTriangular" | custom-call | tf_op jit(solution)/shard_map/jit(cholesky)/cholesky | solution.py:28
  318.9 12.1 %cholesky.162 = f32[128,128]{1,0:T(8,128)S(1)} custom-call(f32[128,128]{1,0:T(8,128)S(1)} %cholesky.196), custom_call_target="Cholesky" | custom-call | tf_op jit(solution)/shard_map/jit(cholesky)/cholesky | solution.py:28
  331.6 9.8 %custom-call.24 = f32[1,128,128]{1,2,0:T(8,128)S(1)} custom-call(f32[1,128,128]{2,1,0:T(8,128)S(1)} %get-tuple-element.33), custom_call_target="InvertDiagBlocksLowerTriangular" | custom-call | tf_op jit(solution)/shard_map/jit(cholesky)/cholesky | solution.py:28
  343.6 11.7 %cholesky.181 = f32[128,128]{1,0:T(8,128)S(1)} custom-call(f32[128,128]{1,0:T(8,128)S(1)} %convolution_subtract_fusion.3), custom_call_target="Cholesky" | custom-call | tf_op jit(solution)/shard_map/jit(cholesky)/cholesky | solution.py:28
  359.2 1.9 select_select_fusion
  361.1 10.2 %while.1 = (s32[]{:T(128)}, f32[384,384]{1,0:T(8,128)}, s32[3,2]{0,1:T(2,128)S(1)}, f32[3,128,128]{2,1,0:T(8,128)}, s32[]{:T(128)}) while((s32[]{:T(128)}, f32[384,384]{1,0:T(8,128)}, s32[3,2]{0,1:T(2,128)S(1)}, f32[3,128,128]{2,1,0:T(8,128)}, s32[]{:T(128)}) %tuple.32), condition=%wide.while_cond, body=%wide.while_body.sunk | while | flops 2 | bytes 132205 | solution.py:29
  361.7 2.9 bitcast_dynamic-update-slice_fusion.2
  365.2 2.8 bitcast_dynamic-update-slice_fusion.2
  368.6 2.8 bitcast_dynamic-update-slice_fusion.2
  371.4 30.5 %custom-call.25 = f32[3,128,128]{1,2,0:T(8,128)S(1)} custom-call(f32[3,128,128]{2,1,0:T(8,128)} %get-tuple-element.10), custom_call_target="InvertDiagBlocksLowerTriangular" | custom-call | tf_op jit(solution)/shard_map/jit(_solve_triangular)/triangular_solve | solution.py:29
  405.0 3.1 convolution_subtract_fusion
  408.9 15.1 %fusion.2 = f32[8,384,4,128]{1,3,2,0:T(8,128)} fusion(f32[8,256,4,128]{3,2,1,0:T(4,128)S(1)} %copy-done.2, f32[384,1024]{1,0:T(8,128)S(1)} %pad_maximum_fusion, s32[]{:T(128)S(6)} %select_n.24), kind=kOutput, calls=%fused_computation.6 | convolution fusion | flops 4831838208 | bytes 10878980 | tf_op jit(solution)/shard_map/xr,sxyz->sryz/dot_general | solution.py:37
  427.6 218.3 %all-reduce.7.cloned.1.call-done = f32[8,384,4,128]{1,3,2,0:T(8,128)} async-done(((f32[8,384,4,128]{1,3,2,0:T(8,128)}), f32[8,384,4,128]{1,3,2,0:T(8,128)}) %all-reduce.7.cloned.1.call-update) | async-done | bytes 6291472
  645.9 2.2 constant_dynamic-slice_fusion.2
  648.0 2.8 copy.23
  (50 shorter events, 24.2 us)
Async XLA Ops:
  7.2 270.0 %copy-start = (f32[1024,384]{1,0:T(8,128)S(1)}, f32[1024,384]{1,0:T(8,128)}, u32[]{:S(2)}) copy-start(f32[1024,384]{1,0:T(8,128)} %param.5) | copy-start | bytes 4718596
  7.2 270.0 %all-reduce.5.cloned.1.call-start = ((), (), s32[]{:S(2)}) async-start(), calls=%async_computation.1 | async-start | bytes 8388608 | tf_op jit(solution)/shard_map/psum | solution.py:22
  19.5 1.9 copy-start.1
  135.9 510.0 %all-reduce.7.cloned.1.call-start = ((), (), s32[]{:S(2)}) async-start(), calls=%async_computation.2 | async-start | bytes 12582912
  292.6 0.8 copy-start.3
  404.3 4.6 copy-start.2
  424.0 0.7 copy-start.4
Sparse Core Ops, SparseCore 0:
  136.0 141.1 all-reduce.4
  424.1 221.7 all-reduce.6
where the time goes:
time: 667 us; the launch traced here: 658 us
  waiting for transfers between devices  359 us (54%)
  blocking collectives  99.2 us (15%)
  other arithmetic  96.4 us (14%)
  matrix products  53.8 us (8%)
  local copies, waits for them, and re-layouts  32.4 us (5%)
  between operations  16.4 us (2%)
    unnamed x3, waiting for transfers between devices  218 us
    psum x1, waiting for transfers between devices, per_device(): lax.psum(jnp.einsum('sxyz,swyz->xw', full_panel, full_panel, precision=hi...  141 us
    all_to_all x1, blocking collectives, per_device(): lax.all_to_all(picked, 'gz', split_axis=2, concat_axis=1, tiled=True)  99.2 us
    another operation x10, other arithmetic, per_device(): lower_factor = jnp.linalg.cholesky(inner_gram)  57.8 us
    another operation x4, other arithmetic, per_device(): jax.scipy.linalg.solve_triangular(lower_factor, image_full.T, lower=True)  32.6 us
    dot_general x1, matrix products, per_device(): projected = jnp.einsum('xr,sxyz->sryz', own_rows, picked, precision=highest)  15.1 us
    dot_general x1, matrix products, per_device(): jnp.einsum('sxyz,swyz->xw', full_panel, full_panel, precision=highest)  14.8 us
  transfers between devices with their start and end apart: 2, of which 2 were waited for; matrix products, arithmetic and copies ran while one was open for 0% of the time, Pallas kernels for 0%

commit v1 on v0

--- a/solution.py
+++ b/solution.py
@@ -20,8 +20,11 @@
     scaling = 1.0 / column_total
     row_share = total_rows // lax.axis_size(("gx", "gy", "gz"))
     gram_full = lax.psum(
-        jnp.einsum("sxyz,swyz->xw", full_panel, full_panel, precision=highest) * scaling,
-        ("gx", "gy", "gz"),
+        lax.psum(
+            jnp.einsum("sxyz,swyz->xw", full_panel, full_panel, precision=highest) * scaling,
+            ("gy", "gz"),
+        ),
+        "gx",
     )
     image_full = jnp.dot(gram_full, basis_start, precision=highest)
     inner_gram = jnp.einsum("xr,xq->rq", image_full, image_full, precision=highest)

time: 667 us -> 747 us (1.12)
  waiting for transfers between devices: 359 us -> 440 us
    psum x0 -> x1, waiting for transfers between devices: none -> 109 us  [per_device(): lax.psum(lax.psum(jnp.einsum('sxyz,swyz->xw', full_panel, full_panel, pre...]
    psum x1, waiting for transfers between devices: 141 us -> 111 us  [per_device(): lax.psum(jnp.einsum('sxyz,swyz->xw', full_panel, full_panel, precision=hi...]
    unnamed x3 -> x4, waiting for transfers between devices: 218 us -> 219 us
  transfers between devices with their start and end apart: 2 -> 3, of which waited for: 2 -> 3; matrix products, arithmetic and copies ran while one was open for 0% -> 0% of each run, Pallas kernels for 0% -> 0%
where the time goes in v1:
time: 747 us; the launch traced here: 738 us
  waiting for transfers between devices  440 us (59%)
  blocking collectives  99.2 us (13%)
  other arithmetic  96.4 us (13%)
  matrix products  53.8 us (7%)
  local copies, waits for them, and re-layouts  32.4 us (4%)
  between operations  16.1 us (2%)
    unnamed x4, waiting for transfers between devices  219 us
    psum x1, waiting for transfers between devices, per_device(): lax.psum(jnp.einsum('sxyz,swyz->xw', full_panel, full_panel, precision=hi...  111 us
    psum x1, waiting for transfers between devices, per_device(): lax.psum(lax.psum(jnp.einsum('sxyz,swyz->xw', full_panel, full_panel, pre...  109 us
    all_to_all x1, blocking collectives, per_device(): lax.all_to_all(picked, 'gz', split_axis=2, concat_axis=1, tiled=True)  99.2 us
    another operation x10, other arithmetic, per_device(): lower_factor = jnp.linalg.cholesky(inner_gram)  57.8 us
    another operation x4, other arithmetic, per_device(): jax.scipy.linalg.solve_triangular(lower_factor, image_full.T, lower=True)  32.6 us
    dot_general x1, matrix products, per_device(): projected = jnp.einsum('xr,sxyz->sryz', own_rows, picked, precision=highest)  15.1 us
  transfers between devices with their start and end apart: 3, of which 3 were waited for; matrix products, arithmetic and copies ran while one was open for 0% of the time, Pallas kernels for 0%

profile of v1, /device:TPU:0, one launch (start us, length us, event | category | flops | bytes accessed | tf_op | source)
XLA Modules:
  0.0 737.7 jit_solution(3390916554980197825)
XLA Ops:
  8.7 7.5 %gather_fusion = f32[8,256,4,128]{3,2,1,0:T(4,128)} fusion(f32[12,256,4,128]{3,2,1,0:T(4,128)} %param.3, s32[1024]{0:T(1024)S(1)} %pad_clamp_fusion), kind=kCustom, calls=%fused_computation | custom fusion | bytes 8388640 | tf_op jit(solution)/shard_map/jit(_take)/gather | solution.py:9
  16.2 3.3 broadcast_select_fusion
  21.4 99.2 %all_to_all.15 = f32[8,256,4,128]{3,1,0,2:T(8,128)S(1)} all-to-all(f32[8,256,4,128]{3,1,0,2:T(8,128)S(1)} %copy.16), channel_id=1, replica_groups=mesh['gx'=2,'gy'=4,'gz'=4] {'gz'}, dimensions={2} | all-to-all | bytes 8388608 | tf_op jit(solution)/shard_map/all_to_all | solution.py:10
  121.1 14.8 %bitcast_multiply_fusion = f32[1024,1024]{1,0:T(8,128)} fusion(f32[8,1024,128]{2,1,0:T(8,128)S(1)} %bitcast.74), kind=kOutput, calls=%fused_computation.3 | convolution fusion | flops 12885950464 | bytes 8388608 | tf_op jit(solution)/shard_map/sxyz,swyz->xw/dot_general | solution.py:24
  135.9 111.0 %all-reduce.6.cloned.1.call-done = f32[1024,1024]{1,0:T(8,128)} async-done(((f32[1024,1024]{1,0:T(8,128)}), f32[1024,1024]{1,0:T(8,128)}) %all-reduce.6.cloned.1.call-update) | async-done | bytes 4194320 | tf_op jit(solution)/shard_map/psum | solution.py:23
  247.1 109.1 %all-reduce.8.cloned.1.call-done = f32[1024,1024]{1,0:T(8,128)} async-done(((f32[1024,1024]{1,0:T(8,128)}), f32[1024,1024]{1,0:T(8,128)}) %all-reduce.8.cloned.1.call-update) | async-done | bytes 4194320 | tf_op jit(solution)/shard_map/psum | solution.py:22
  356.3 8.5 %fusion.27 = f32[1024,384]{1,0:T(8,128)S(1)} fusion(f32[1024,1024]{1,0:T(8,128)} %all-reduce.8.cloned.1.call-done, f32[1024,384]{1,0:T(8,128)S(1)} %copy-done), kind=kOutput, calls=%fused_computation.62 | convolution fusion | flops 4831838208 | bytes 7340032 | tf_op jit(solution)/shard_map/dot_general | solution.py:29
  364.8 3.5 fusion.28
  368.3 2.1 copy.18
  372.5 11.7 %cholesky.77 = f32[128,128]{1,0:T(8,128)S(1)} custom-call(f32[128,128]{1,0:T(8,128)S(1)} %cholesky.192), custom_call_target="Cholesky" | custom-call | tf_op jit(solution)/shard_map/jit(cholesky)/cholesky | solution.py:31
  385.2 9.8 %custom-call.23 = f32[1,128,128]{1,2,0:T(8,128)S(1)} custom-call(f32[1,128,128]{2,1,0:T(8,128)S(1)} %get-tuple-element.36), custom_call_target="InvertDiagBlocksLowerTriangular" | custom-call | tf_op jit(solution)/shard_map/jit(cholesky)/cholesky | solution.py:31
  398.0 12.1 %cholesky.162 = f32[128,128]{1,0:T(8,128)S(1)} custom-call(f32[128,128]{1,0:T(8,128)S(1)} %cholesky.196), custom_call_target="Cholesky" | custom-call | tf_op jit(solution)/shard_map/jit(cholesky)/cholesky | solution.py:31
  410.7 9.8 %custom-call.24 = f32[1,128,128]{1,2,0:T(8,128)S(1)} custom-call(f32[1,128,128]{2,1,0:T(8,128)S(1)} %get-tuple-element.33), custom_call_target="InvertDiagBlocksLowerTriangular" | custom-call | tf_op jit(solution)/shard_map/jit(cholesky)/cholesky | solution.py:31
  422.6 11.7 %cholesky.181 = f32[128,128]{1,0:T(8,128)S(1)} custom-call(f32[128,128]{1,0:T(8,128)S(1)} %convolution_subtract_fusion.3), custom_call_target="Cholesky" | custom-call | tf_op jit(solution)/shard_map/jit(cholesky)/cholesky | solution.py:31
  440.2 10.2 %while.1 = (s32[]{:T(128)}, f32[384,384]{1,0:T(8,128)}, s32[3,2]{0,1:T(2,128)S(1)}, f32[3,128,128]{2,1,0:T(8,128)}, s32[]{:T(128)}) while((s32[]{:T(128)}, f32[384,384]{1,0:T(8,128)}, s32[3,2]{0,1:T(2,128)S(1)}, f32[3,128,128]{2,1,0:T(8,128)}, s32[]{:T(128)}) %tuple.32), condition=%wide.while_cond, body=%wide.while_body.sunk | while | flops 2 | bytes 132205 | solution.py:32
  440.8 2.9 bitcast_dynamic-update-slice_fusion.2
  444.2 2.8 bitcast_dynamic-update-slice_fusion.2
  447.7 2.8 bitcast_dynamic-update-slice_fusion.2
  450.4 30.5 %custom-call.25 = f32[3,128,128]{1,2,0:T(8,128)S(1)} custom-call(f32[3,128,128]{2,1,0:T(8,128)} %get-tuple-element.10), custom_call_target="InvertDiagBlocksLowerTriangular" | custom-call | tf_op jit(solution)/shard_map/jit(_solve_triangular)/triangular_solve | solution.py:32
  484.1 3.1 convolution_subtract_fusion
  488.0 15.1 %fusion.2 = f32[8,384,4,128]{1,3,2,0:T(8,128)} fusion(f32[8,256,4,128]{3,2,1,0:T(4,128)S(1)} %copy-done.2, f32[384,1024]{1,0:T(8,128)S(1)} %pad_maximum_fusion, s32[]{:T(128)S(6)} %select_n.24), kind=kOutput, calls=%fused_computation.6 | convolution fusion | flops 4831838208 | bytes 10878980 | tf_op jit(solution)/shard_map/xr,sxyz->sryz/dot_general | solution.py:40
  506.7 219.4 %all-reduce.10.cloned.1.call-done = f32[8,384,4,128]{1,3,2,0:T(8,128)} async-done(((f32[8,384,4,128]{1,3,2,0:T(8,128)}), f32[8,384,4,128]{1,3,2,0:T(8,128)}) %all-reduce.10.cloned.1.call-update) | async-done | bytes 6291472
  726.1 2.2 constant_dynamic-slice_fusion.2
  728.3 2.8 copy.23
  (53 shorter events, 26.2 us)
Async XLA Ops:
  7.2 349.1 %copy-start = (f32[1024,384]{1,0:T(8,128)S(1)}, f32[1024,384]{1,0:T(8,128)}, u32[]{:S(2)}) copy-start(f32[1024,384]{1,0:T(8,128)} %param.5) | copy-start | bytes 4718596
  7.2 239.7 %all-reduce.6.cloned.1.call-start = ((), (), s32[]{:S(2)}) async-start(), calls=%async_computation.1 | async-start | bytes 8388608 | tf_op jit(solution)/shard_map/psum | solution.py:23
  19.5 1.9 copy-start.1
  135.9 220.4 %all-reduce.8.cloned.1.call-start = ((), (), s32[]{:S(2)}) async-start(), calls=%async_computation.2 | async-start | bytes 8388608 | tf_op jit(solution)/shard_map/psum | solution.py:22
  246.9 479.2 %all-reduce.10.cloned.1.call-start = ((), (), s32[]{:S(2)}) async-start(), calls=%async_computation.3 | async-start | bytes 12582912
  371.7 0.8 copy-start.3
  483.4 4.6 copy-start.2
  503.0 0.7 copy-start.4
Sparse Core Ops, SparseCore 0:
  136.0 110.8 all-reduce.5
  249.4 106.7 all-reduce.7
  503.2 222.8 all-reduce.9
